TPU v7x, 128 devices: a whole 4x4x4 slice. The times are simulated.
128 devices in a mesh: dp: 64 (over z, y, x), expert: 2 (over core).
Axes of the slice: x: 4, y: 4, z: 4, core: 2. Of those that a mesh axis runs over, the one named last changes fastest.
Arguments:
- hidden: bfloat16 [2, 65536, 1024], P('expert', 'dp'), may hold values from -6 to 6
- cotangent: bfloat16 [2, 65536, 3584], P('expert', 'dp'), may hold values from -6 to 6
- counts: int32 [2, 64], P('expert', 'dp'), may hold values from 1 to 1024, as said below
- placement: int32 [2, 4], replicated, may hold values from 0 to 1, as said below
- weight: bfloat16 [2, 1024, 3584], P('expert', 'dp'), may hold values from -4 to 4
- moment: float32 [2, 1024, 3584], P('expert', 'dp'), may hold values from -2 to 2
- second: float32 [2, 1024, 3584], P('expert', 'dp'), may hold values from 0.005 to 1
- serving: bfloat16 [2, 4, 1024, 3584], P('expert', None, 'dp'), may hold values from -4 to 4
Outputs:
- d_hidden: bfloat16 [2, 65536, 1024], P('expert', 'dp')
- new_weight: bfloat16 [2, 1024, 3584], P('expert', 'dp')
- new_moment: float32 [2, 1024, 3584], P('expert', 'dp')
- new_second: float32 [2, 1024, 3584], P('expert', 'dp')
- served: bfloat16 [2, 4, 1024, 3584], P('expert', None, 'dp')
Inputs may be any that keep to these rules, and one draw needn't show every extreme that they name: `counts`: every count is reached by some expert and data shard in every draw at its upper end, 1024. `placement`: some two groups hold different experts as their first replica.
All inputs are finite; a program needn't handle non-finite values.
Results may differ from a plain program's by a relative error of at most 0.0012.
Values may be sent and summed in bfloat16 or wider, within the bound.
A program may use at most 128 MiB of HBM per device.

v0:
```python
import jax
import jax.numpy as jnp
from jax import lax
from jax.sharding import Mesh
from jax.sharding import PartitionSpec as P

D = 3584
DP = ("dp_0", "dp_1", "dp_2")
beta_one = 0.9
beta_two = 0.95
bias_one = 1.0 - 0.9**20
bias_two = 1.0 - 0.95**20
learn_rate = 0.05
decay_rate = 0.1
epsilon = 1e-08


def summed_rows(array, axes, dim):
    if not axes:
        return array
    nearer = lax.psum_scatter(array, axes[0], scatter_dimension=dim, tiled=True)
    return summed_rows(nearer, axes[1:], dim)


def on_device(hidden, cotangent, counts, placement, weight, moment, second, serving):
    scale = D ** (-0.5)
    acts = hidden[0]
    grads_out = cotangent[0]
    matrix = weight[0]
    tokens = acts.shape[0]
    owned = matrix.shape[0]
    width = matrix.shape[1]
    live = jnp.arange(tokens, dtype=jnp.int32) < counts[0, 0]
    masked = jnp.where(live[:, None], grads_out, jnp.zeros_like(grads_out))
    d_full = scale * jnp.dot(
        masked, lax.all_gather(matrix, DP, axis=0, tiled=True).T, preferred_element_type=jnp.float32
    )
    d_hid = d_full.astype(jnp.bfloat16)
    full_term = scale * jnp.dot(acts.T, masked, preferred_element_type=jnp.float32)
    grad = summed_rows(full_term, DP, 0)
    first_new = beta_one * moment[0] + (1.0 - beta_one) * grad
    squares_new = beta_two * second[0] + (1.0 - beta_two) * grad * grad
    step = first_new / bias_one / (jnp.sqrt(squares_new / bias_two) + epsilon)
    current = matrix.astype(jnp.float32)
    updated = current - learn_rate * (step + decay_rate * current)
    delta = (updated - current).astype(jnp.bfloat16)
    groups = lax.axis_size("expert")
    flat = delta.reshape(groups, -1)
    spread = lax.all_to_all(flat, "expert", split_axis=0, concat_axis=0, tiled=True)
    chosen = jnp.take(spread, placement.T, axis=0)
    arrived = lax.all_to_all(chosen, "expert", split_axis=1, concat_axis=1, tiled=True)
    copies = arrived.shape[0]
    incoming = arrived.reshape(copies, owned, width)
    served = (serving[0].astype(jnp.float32) + incoming.astype(jnp.float32)).astype(jnp.bfloat16)
    return (
        d_hid[None],
        updated.astype(jnp.bfloat16)[None],
        first_new[None],
        squares_new[None],
        served[None],
    )


def solution(mesh):
    torus = Mesh(
        mesh.devices.reshape(4, 4, 4, mesh.shape["expert"]), ("dp_0", "dp_1", "dp_2", "expert")
    )
    return jax.shard_map(
        on_device,
        mesh=torus,
        in_specs=(
            P("expert", DP, None),
            P("expert", DP, None),
            P("expert", DP),
            P(),
            P("expert", DP, None),
            P("expert", DP, None),
            P("expert", DP, None),
            P("expert", None, DP, None),
        ),
        out_specs=(
            P("expert", DP, None),
            P("expert", DP, None),
            P("expert", DP, None),
            P("expert", DP, None),
            P("expert", None, DP, None),
        ),
        check_vma=False,
    )
```

profile of v0, /device:TPU:1, one launch (start us, length us, event | category | flops | bytes accessed | tf_op | source)
XLA Modules:
  0.0 302.0 jit_solution(9500016079672712635)
XLA Ops:
  8.0 0.0 copy-start
  8.0 0.0 reduce-scatter.8.cloned.1.call-start
  8.9 0.8 copy-done
  9.6 14.4 %multiply_bitcast_fusion = f32[1024,3584]{0,1:T(8,128)} fusion(bf16[1,1024,3584]{2,1,0:T(8,128)(2,1)} %param.9, pred[1024]{0:T(1024)(128)(4,1)S(1)} %iota_compare_fusion, bf16[1,1024,1024]{2,1,0:T(8,128)(2,1)S(1)} %copy-done), kind=kOutput, calls=%fused_computation.1 | convolution fusion | flops 7523532800 | bytes 24118272 | tf_op jit(solution)/shard_map/dot_general | solution.py:39
  24.0 0.0 reduce-scatter.8.cloned.1.call-update
  24.0 0.0 copy-start.4
  24.0 0.0 reduce-scatter.10.cloned.1.call-start
  24.1 135.1 %reduce-scatter.8.cloned.1.call-done = f32[256,3584]{0,1:T(8,128)} async-done(((f32[1024,3584]{0,1:T(8,128)}), f32[256,3584]{0,1:T(8,128)}) %reduce-scatter.8.cloned.1.call-update) | async-done | bytes 3670032 | tf_op jit(solution)/shard_map/reduce_scatter | solution.py:21
  159.1 5.2 %copy.58 = f32[256,3584]{1,0:T(8,128)} copy(f32[256,3584]{0,1:T(8,128)} %reduce-scatter.8.cloned.1.call-done) | data formatting | bytes 7340032
  164.3 0.0 reduce-scatter.10.cloned.1.call-update
  164.3 0.0 all-gather.3.cloned.1.call-start
  164.4 0.5 all-gather.3.cloned.1.call-update
  164.9 0.0 reduce-scatter.12.cloned.1.call-start
  165.0 0.0 copy-done.4
  165.0 0.1 copy.55
  165.1 0.1 reshape.51
  165.2 42.3 %reduce-scatter.10.cloned.1.call-done = f32[64,3584]{1,0:T(8,128)} async-done(((f32[256,3584]{1,0:T(8,128)}), f32[64,3584]{1,0:T(8,128)}) %reduce-scatter.10.cloned.1.call-update) | async-done | bytes 917520
  207.4 0.0 reduce-scatter.12.cloned.1.call-update
  207.5 0.0 copy-start.1
  207.5 0.0 copy-start.2
  207.5 0.0 copy-start.3
  207.5 54.5 %all-gather.3.cloned.1.call-done = bf16[1,1024,3584]{2,1,0:T(8,128)(2,1)} async-done(((bf16[1,16,3584]{2,1,0:T(8,128)(2,1)}), bf16[1,1024,3584]{2,1,0:T(8,128)(2,1)}) %all-gather.3.cloned.1.call-update) | async-done | bytes 7340048 | tf_op jit(solution)/shard_map/all_gather | solution.py:36
  262.0 13.2 %fusion.11 = bf16[1,1024,1024]{2,1,0:T(8,128)(2,1)} fusion(bf16[1,1024,3584]{2,1,0:T(8,128)(2,1)} %all-gather.3.cloned.1.call-done, bf16[1,1024,3584]{2,1,0:T(8,128)(2,1)} %param.9, pred[1024]{0:T(1024)(128)(4,1)S(1)} %iota_compare_fusion), kind=kOutput, calls=%fused_computation.13 | convolution fusion | flops 7521959936 | bytes 16778240 | tf_op jit(solution)/shard_map/dot_general | solution.py:35
  275.2 0.0 reduce-scatter.12.cloned.1.call-done
  275.2 0.0 copy-done.1
  275.2 0.0 copy-done.2
  275.2 0.0 copy-done.3
  275.2 1.9 fusion.17
  277.1 0.1 all_to_all.15
  277.1 0.5 broadcast.53
  277.7 1.4 reduce
  279.1 0.1 reshape.65
  279.2 4.3 %all_to_all.18 = bf16[2,2,14336]{2,1,0:T(2,128)(2,1)S(1)} all-to-all(bf16[2,2,14336]{2,1,0:T(2,128)(2,1)S(1)} %reshape.65), channel_id=1, replica_groups=mesh['dp_0'=4,'dp_1'=4,'dp_2'=4,'expert'=2] {'expert'}, dimensions={0} | all-to-all | bytes 229376 | tf_op jit(solution)/shard_map/all_to_all | solution.py:49
  283.4 0.1 reshape.66
  283.6 0.2 copy.65
  283.7 0.8 gather_fusion
  284.6 0.3 reshape.50
  284.9 0.6 copy_select_fusion
  285.5 4.1 %all_to_all.19 = bf16[4,2,28672]{2,0,1:T(4,128)(2,1)S(1)} all-to-all(bf16[4,2,28672]{2,0,1:T(4,128)(2,1)S(1)} %copy_select_fusion), channel_id=1, replica_groups=mesh['dp_0'=4,'dp_1'=4,'dp_2'=4,'expert'=2] {'expert'}, dimensions={1} | all-to-all | bytes 917504 | tf_op jit(solution)/shard_map/all_to_all | solution.py:51
  289.6 1.4 copy.57
  291.0 2.0 reshape.48
  293.0 1.9 add_convert_fusion
  (4 shorter events, 0.0 us)
Async XLA Ops:
  8.0 1.6 copy-start
  8.0 151.1 %reduce-scatter.8.cloned.1.call-start = ((), (), s32[]{:S(2)}) async-start(), calls=%async_computation.5 | async-start | bytes 18350080 | tf_op jit(solution)/shard_map/reduce_scatter | solution.py:21
  24.0 140.9 %copy-start.4 = (s32[2,4]{1,0:T(2,128)S(1)}, s32[2,4]{1,0:T(2,128)}, u32[]{:S(2)}) copy-start(s32[2,4]{1,0:T(2,128)} %param.11) | copy-start | bytes 100
  24.0 183.4 %reduce-scatter.10.cloned.1.call-start = ((), (), s32[]{:S(2)}) async-start(), calls=%async_computation.7 | async-start | bytes 4587520
  164.3 97.7 %all-gather.3.cloned.1.call-start = ((), (), s32[]{:S(2)}) async-start(), calls=%async_computation.6 | async-start | bytes 7454720 | tf_op jit(solution)/shard_map/all_gather | solution.py:36
  164.9 110.3 %reduce-scatter.12.cloned.1.call-start = ((), (), s32[]{:S(2)}) async-start(), calls=%async_computation.8 | async-start | bytes 1146880 | tf_op jit(solution)/shard_map/reduce_scatter | solution.py:21
  207.5 67.7 %copy-start.1 = (bf16[1,16,3584]{2,1,0:T(8,128)(2,1)S(1)}, bf16[1,16,3584]{2,1,0:T(8,128)(2,1)}, u32[]{:S(2)}) copy-start(bf16[1,16,3584]{2,1,0:T(8,128)(2,1)} %param.12) | copy-start | bytes 344068
  207.5 67.7 %copy-start.2 = (f32[1,16,3584]{2,1,0:T(8,128)S(1)}, f32[1,16,3584]{2,1,0:T(8,128)}, u32[]{:S(2)}) copy-start(f32[1,16,3584]{2,1,0:T(8,128)} %param.14) | copy-start | bytes 688132
  207.5 67.7 %copy-start.3 = (f32[1,16,3584]{2,1,0:T(8,128)S(1)}, f32[1,16,3584]{2,1,0:T(8,128)}, u32[]{:S(2)}) copy-start(f32[1,16,3584]{2,1,0:T(8,128)} %param.13) | copy-start | bytes 688132
Sparse Core Ops, SparseCore 0:
  24.1 134.9 reduce-scatter.7
  164.5 42.9 reduce-scatter.9
  209.9 22.5 reduce-scatter.11
Sparse Core Ops, SparseCore 1:
  167.6 94.4 all-gather.2
where the time goes:
time: 302 us
  waiting for transfers between devices  232 us (77%)
  matrix products  27.6 us (9%)
  between operations  16.1 us (5%)
  local copies, waits for them, and re-layouts  11.6 us (4%)
  blocking collectives  8.34 us (3%)
  other arithmetic  5.8 us (2%)
    reduce_scatter x2, waiting for transfers between devices, summed_rows(): nearer = lax.psum_scatter(array, axes[0], scatter_dimension=dim, tiled=True)  135 us
    all_gather x1, waiting for transfers between devices, on_device(): lax.all_gather(matrix, DP, axis=0, tiled=True)  54.5 us
    unnamed x5, waiting for transfers between devices  42.8 us
    dot_general x1, matrix products, on_device(): jnp.dot(acts.T, masked, preferred_element_type=jnp.float32)  14.4 us
    dot_general x1, matrix products, on_device(): jnp.dot(masked, lax.all_gather(matrix, DP, axis=0, tiled=True).T, preferr...  13.2 us
    unnamed x14, local copies, waits for them, and re-layouts  6.33 us
  transfers between devices with their start and end apart: 4, of which 3 were waited for; matrix products, arithmetic and copies ran while one was open for 4% of the time, Pallas kernels for 0%

commit v1 on v0

--- a/solution.py
+++ b/solution.py
@@ -13,6 +13,11 @@
 learn_rate = 0.05
 decay_rate = 0.1
 epsilon = 1e-08
+
+
+def exchange_gather(array, axis, dim):
+    sent = jnp.stack([array] * lax.axis_size(axis))
+    return jnp.concatenate(lax.all_to_all(sent, axis, 0, 0), axis=dim)
 
 
 def summed_rows(array, axes, dim):
@@ -33,7 +38,7 @@
     live = jnp.arange(tokens, dtype=jnp.int32) < counts[0, 0]
     masked = jnp.where(live[:, None], grads_out, jnp.zeros_like(grads_out))
     d_full = scale * jnp.dot(
-        masked, lax.all_gather(matrix, DP, axis=0, tiled=True).T, preferred_element_type=jnp.float32
+        masked, exchange_gather(matrix, DP, 0).T, preferred_element_type=jnp.float32
     )
     d_hid = d_full.astype(jnp.bfloat16)
     full_term = scale * jnp.dot(acts.T, masked, preferred_element_type=jnp.float32)

time: 302 us -> 343 us (1.14)
  waiting for transfers between devices: 232 us -> 260 us
  starting transfers between devices: 0.17 us -> 8.82 us
  local copies, waits for them, and re-layouts: 11.6 us -> 15.5 us
    unnamed x5 -> x4, waiting for transfers between devices: 42.8 us -> 116 us
    all_gather x1 -> x0, waiting for transfers between devices: 54.5 us -> none  [on_device(): lax.all_gather(matrix, DP, axis=0, tiled=True)]
    reduce_scatter x2, waiting for transfers between devices: 135 us -> 144 us  [summed_rows(): nearer = lax.psum_scatter(array, axes[0], scatter_dimension=dim, tiled=True)]
    all_to_all x0 -> x1, starting transfers between devices: none -> 8.7 us  [exchange_gather(): return jnp.concatenate(lax.all_to_all(sent, axis, 0, 0), axis=dim)]
    another operation x0 -> x1, local copies, waits for them, and re-layouts: none -> 3.9 us  [exchange_gather(): sent = jnp.stack([array] * lax.axis_size(axis))]
  transfers between devices with their start and end apart: 4 -> 4, of which waited for: 3 -> 3; matrix products, arithmetic and copies ran while one was open for 4% -> 5% of each run, Pallas kernels for 0% -> 0%
where the time goes in v1:
time: 343 us; the launch traced here: 342 us
  waiting for transfers between devices  260 us (76%)
  matrix products  27.6 us (8%)
  local copies, waits for them, and re-layouts  15.5 us (5%)
  between operations  14.7 us (4%)
  blocking collectives  9.92 us (3%)
  starting transfers between devices  8.82 us (3%)
  other arithmetic  5.79 us (2%)
    reduce_scatter x2, waiting for transfers between devices, summed_rows(): nearer = lax.psum_scatter(array, axes[0], scatter_dimension=dim, tiled=True)  144 us
    unnamed x4, waiting for transfers between devices  116 us
    dot_general x1, matrix products, on_device(): jnp.dot(acts.T, masked, preferred_element_type=jnp.float32)  14.4 us
    dot_general x1, matrix products, on_device(): jnp.dot(masked, exchange_gather(matrix, DP, 0).T, preferred_element_type=...  13.2 us
    all_to_all x1, starting transfers between devices, exchange_gather(): return jnp.concatenate(lax.all_to_all(sent, axis, 0, 0), axis=dim)  8.7 us
  transfers between devices with their start and end apart: 4, of which 3 were waited for; matrix products, arithmetic and copies ran while one was open for 5% of the time, Pallas kernels for 0%

profile of v1, /device:TPU:1, one launch (start us, length us, event | category | flops | bytes accessed | tf_op | source)
XLA Modules:
  0.0 342.5 jit_solution(6336566225699425201)
XLA Ops:
  7.2 0.0 copy-start
  7.2 0.0 reduce-scatter.8.cloned.1.call-start
  8.0 0.8 copy-done
  8.8 14.4 %multiply_bitcast_fusion = f32[1024,3584]{0,1:T(8,128)} fusion(bf16[1,1024,3584]{2,1,0:T(8,128)(2,1)} %param.9, pred[1024]{0:T(1024)(128)(4,1)S(1)} %iota_compare_fusion, bf16[1,1024,1024]{2,1,0:T(8,128)(2,1)S(1)} %copy-done), kind=kOutput, calls=%fused_computation.1 | convolution fusion | flops 7523532800 | bytes 24118272 | tf_op jit(solution)/shard_map/dot_general | solution.py:44
  23.2 0.0 reduce-scatter.8.cloned.1.call-update
  23.2 0.0 copy-start.1
  23.2 0.0 reduce-scatter.10.cloned.1.call-start
  23.2 135.1 %reduce-scatter.8.cloned.1.call-done = f32[256,3584]{0,1:T(8,128)} async-done(((f32[1024,3584]{0,1:T(8,128)}), f32[256,3584]{0,1:T(8,128)}) %reduce-scatter.8.cloned.1.call-update) | async-done | bytes 3670032 | tf_op jit(solution)/shard_map/reduce_scatter | solution.py:26
  158.3 5.1 %copy.62 = f32[256,3584]{1,0:T(8,128)} copy(f32[256,3584]{0,1:T(8,128)} %reduce-scatter.8.cloned.1.call-done) | data formatting | bytes 7340032
  163.4 0.0 reduce-scatter.10.cloned.1.call-update
  163.5 0.0 copy-done.1
  163.5 3.9 %stack.3 = bf16[64,16,3584]{2,1,0:T(8,128)(2,1)} broadcast(bf16[16,3584]{1,0:T(8,128)(2,1)S(1)} %bitcast.53), dimensions={1,2} | broadcast | bytes 7454720 | tf_op jit(solution)/shard_map/stack | solution.py:19
  167.4 0.0 copy-start.4
  167.4 8.7 %all-to-all-start = ((bf16[64,16,3584]{2,1,0:T(8,128)(2,1)}), bf16[64,16,3584]{2,1,0:T(8,128)(2,1)}, u32[]{:S(2)}, u32[]{:S(2)}) async-start(bf16[64,16,3584]{2,1,0:T(8,128)(2,1)} %stack.3), calls=%async_computation | async-start | bytes 14680064 | tf_op jit(solution)/shard_map/all_to_all | solution.py:20
  176.1 0.0 reduce-scatter.12.cloned.1.call-start
  176.1 0.0 copy-done.4
  176.2 0.1 copy.59
  176.2 0.1 reshape.64
  176.3 115.8 %reduce-scatter.10.cloned.1.call-done = f32[64,3584]{1,0:T(8,128)} async-done(((f32[256,3584]{1,0:T(8,128)}), f32[64,3584]{1,0:T(8,128)}) %reduce-scatter.10.cloned.1.call-update) | async-done | bytes 917520
  292.2 0.0 reduce-scatter.12.cloned.1.call-update
  292.2 0.0 all-to-all-done
  292.2 0.0 copy-start.2
  292.2 0.0 copy-start.3
  292.3 13.2 %fusion.3 = bf16[1,1024,1024]{2,1,0:T(8,128)(2,1)} fusion(bf16[1024,3584]{1,0:T(8,128)(2,1)} %bitcast.3, bf16[1,1024,3584]{2,1,0:T(8,128)(2,1)} %param.9, pred[1024]{0:T(1024)(128)(4,1)S(1)} %iota_compare_fusion), kind=kOutput, calls=%fused_computation.7 | convolution fusion | flops 7521959936 | bytes 16778240 | tf_op jit(solution)/shard_map/dot_general | solution.py:40
  305.5 9.2 %reduce-scatter.12.cloned.1.call-done = f32[16,3584]{1,0:T(8,128)} async-done(((f32[64,3584]{1,0:T(8,128)}), f32[16,3584]{1,0:T(8,128)}) %reduce-scatter.12.cloned.1.call-update) | async-done | bytes 229392 | tf_op jit(solution)/shard_map/reduce_scatter | solution.py:26
  314.7 0.0 copy-done.2
  314.7 0.0 copy-done.3
  314.7 1.9 fusion.9
  316.6 0.1 all_to_all.19
  316.6 0.5 broadcast.58
  317.2 1.4 reduce
  318.6 0.1 reshape.76
  318.7 5.8 %all_to_all.23 = bf16[2,2,14336]{2,1,0:T(2,128)(2,1)S(1)} all-to-all(bf16[2,2,14336]{2,1,0:T(2,128)(2,1)S(1)} %reshape.76), channel_id=1, replica_groups=mesh['dp_0'=4,'dp_1'=4,'dp_2'=4,'expert'=2] {'expert'}, dimensions={0} | all-to-all | bytes 229376 | tf_op jit(solution)/shard_map/all_to_all | solution.py:54
  324.5 0.1 reshape.77
  324.6 0.2 copy.69
  324.8 0.8 gather_fusion
  325.7 0.3 reshape.63
  326.0 0.6 copy_select_fusion
  326.6 4.1 %all_to_all.24 = bf16[4,2,28672]{2,0,1:T(4,128)(2,1)S(1)} all-to-all(bf16[4,2,28672]{2,0,1:T(4,128)(2,1)S(1)} %copy_select_fusion), channel_id=1, replica_groups=mesh['dp_0'=4,'dp_1'=4,'dp_2'=4,'expert'=2] {'expert'}, dimensions={1} | all-to-all | bytes 917504 | tf_op jit(solution)/shard_map/all_to_all | solution.py:56
  330.7 1.4 copy.61
  332.1 2.0 reshape.61
  334.1 1.9 add_convert_fusion
  (4 shorter events, 0.0 us)
Async XLA Ops:
  7.2 1.6 copy-start
  7.2 151.1 %reduce-scatter.8.cloned.1.call-start = ((), (), s32[]{:S(2)}) async-start(), calls=%async_computation.6 | async-start | bytes 18350080 | tf_op jit(solution)/shard_map/reduce_scatter | solution.py:26
  23.2 140.3 %copy-start.1 = (bf16[1,16,3584]{2,1,0:T(8,128)(2,1)S(1)}, bf16[1,16,3584]{2,1,0:T(8,128)(2,1)}, u32[]{:S(2)}) copy-start(bf16[1,16,3584]{2,1,0:T(8,128)(2,1)} %param.12) | copy-start | bytes 344068
  23.2 269.0 %reduce-scatter.10.cloned.1.call-start = ((), (), s32[]{:S(2)}) async-start(), calls=%async_computation.7 | async-start | bytes 4587520
  167.4 8.8 %copy-start.4 = (s32[2,4]{1,0:T(2,128)S(1)}, s32[2,4]{1,0:T(2,128)}, u32[]{:S(2)}) copy-start(s32[2,4]{1,0:T(2,128)} %param.11) | copy-start | bytes 100
  167.4 124.9 %all-to-all-start = ((bf16[64,16,3584]{2,1,0:T(8,128)(2,1)}), bf16[64,16,3584]{2,1,0:T(8,128)(2,1)}, u32[]{:S(2)}, u32[]{:S(2)}) async-start(bf16[64,16,3584]{2,1,0:T(8,128)(2,1)} %stack.3), calls=%async_computation | async-start | bytes 14680064 | tf_op jit(solution)/shard_map/all_to_all | solution.py:20
  176.1 138.6 %reduce-scatter.12.cloned.1.call-start = ((), (), s32[]{:S(2)}) async-start(), calls=%async_computation.8 | async-start | bytes 1146880 | tf_op jit(solution)/shard_map/reduce_scatter | solution.py:26
  292.2 22.5 %copy-start.2 = (f32[1,16,3584]{2,1,0:T(8,128)S(1)}, f32[1,16,3584]{2,1,0:T(8,128)}, u32[]{:S(2)}) copy-start(f32[1,16,3584]{2,1,0:T(8,128)} %param.14) | copy-start | bytes 688132
  292.2 22.5 %copy-start.3 = (f32[1,16,3584]{2,1,0:T(8,128)S(1)}, f32[1,16,3584]{2,1,0:T(8,128)}, u32[]{:S(2)}) copy-start(f32[1,16,3584]{2,1,0:T(8,128)} %param.13) | copy-start | bytes 688132
Sparse Core Ops, SparseCore 0:
  23.3 134.9 reduce-scatter.7
  163.6 128.5 reduce-scatter.9
  294.6 20.0 reduce-scatter.11
